TPU v7x, 512 devices: a whole 4x8x8 slice. The times are simulated.
512 devices in a mesh: sub: 128 (over y, z, core), grp: 4 (over x).
Axes of the slice: x: 4, y: 8, z: 8, core: 2. Of those that a mesh axis runs over, the one named last changes fastest.
Arguments:
- lam_start: float32 [524288, 128], P(('sub', 'grp')), may hold values from -6 to 6
- loads: float32 [524288, 128], P(('sub', 'grp')), may hold values from -40 to 40
- dual_ops: bfloat16 [512, 1024, 1024], P(('sub', 'grp')), may hold values from -40 to 40, as said below
- modes: float32 [6, 524288], P(None, ('sub', 'grp')), may hold values from -0.6 to 0.6
- coarse_inverse: float32 [3072, 3072], P('sub', 'grp'), may hold values from -1 to 1, as said below
- face_offset: int32 [128, 4, 8], P(None, 'grp'), may hold values from 0 to 3, as said below
- face_block: int32 [128, 4, 8], P(None, 'grp'), may hold values from 0 to 7
- face_sign: int32 [128, 4, 8], P(None, 'grp'), may hold values from 0 to 1
- contact: int32 [3, 524288], P(None, ('sub', 'grp')), may hold values 0 or 1
Outputs:
- multipliers: float32 [524288, 128], P(('sub', 'grp'))
Inputs may be any that keep to these rules, and one draw needn't show every extreme that they name: Each block dual_ops[k] is symmetric positive definite. coarse_inverse is symmetric positive definite. `face_offset`: no face reads from outside the order 0 to 127. For every subdomain no value is taken by more than 4 of its faces, and exactly 4 of its faces share one value.
All inputs are finite; a program needn't handle non-finite values. No bound on the sum of `contact` on one device may be relied on, other than what follows from the above.
Results may differ from a plain program's by a relative error of at most 0.005.
Values may be sent and summed in bfloat16 or wider, within the bound.
A program may use at most 64 MiB of HBM per device.

v0:
```python
import jax
import jax.numpy as jnp
from jax import lax
from jax.sharding import Mesh
from jax.sharding import PartitionSpec as P

FACES = 8
FACE_ROWS = 32
CAP = 4
MODES = 6
STEPS = 3
SUB = ("sub_0", "sub_1", "sub_2")
SUB_GRP = ("sub_0", "sub_1", "sub_2", "grp")


def passed_along(value, axis, steps):
    count = lax.axis_size(axis)
    leading, last = (max(0, -steps), min(count, count - steps))
    return lax.ppermute(value, axis, [(source, source + steps) for source in range(leading, last)])


def cut_along(x, dim, length):
    lengths = x.shape
    parts = x.reshape(*lengths[:dim], length, lengths[dim] // length, *lengths[dim + 1 :])
    return jnp.moveaxis(parts, dim, 0)


def sum_at_owner(x, axis, dim):
    length = lax.axis_size(axis)
    parts = lax.all_to_all(cut_along(x, dim, length), axis, 0, 0, tiled=True)
    return jnp.sum(parts, axis=0)


def over_axes(x, axes):
    for axis in axes:
        x = lax.psum(x, axis)
    return x


def own_row(table, index):
    return lax.dynamic_index_in_dim(table[:, 0, :], index, 0, keepdims=False)


def slot_matrix(offsets, which):
    match = (offsets == which).astype(jnp.int32)
    rank = jnp.cumsum(match) - 1
    picked = (rank[:, None] == jnp.arange(CAP, dtype=jnp.int32)[None, :]) & (match[:, None] == 1)
    return picked.astype(jnp.float32)


def build_tables(face_offset, face_block, face_sign):
    sub_here = lax.axis_index(SUB)
    sub_count = lax.axis_size(SUB)
    offs_own = own_row(face_offset, sub_here)
    sign_own = (2 * own_row(face_sign, sub_here) - 1).astype(jnp.float32)
    block_ids = jnp.arange(FACES, dtype=jnp.int32)
    tables = []
    for which, moved in enumerate((-2, -1, 1, 2)):
        reader = jnp.clip(sub_here - moved, 0, sub_count - 1)
        offs_far = own_row(face_offset, reader)
        blocks_far = own_row(face_block, reader)
        sign_far = (2 * own_row(face_sign, reader) - 1).astype(jnp.float32)
        onehot_far = (blocks_far[:, None] == block_ids[None, :]).astype(jnp.float32)
        sel_own = slot_matrix(offs_own, which)
        sel_far = slot_matrix(offs_far, which)
        pack = jnp.dot(sel_far.T, onehot_far).astype(jnp.bfloat16)
        place = (sel_own * sign_own[:, None]).astype(jnp.bfloat16)
        unpack = jnp.dot((sel_far * sign_far[:, None]).T, onehot_far).astype(jnp.bfloat16)
        tables.append((moved, pack, place, sel_own.astype(jnp.bfloat16), unpack))
    return tables


def apply_dual(field, dual_ops, tables):
    normal_loads = field.shape[-1]
    face_total = FACES * FACE_ROWS
    low = field.astype(jnp.bfloat16)
    faces = low[:face_total].reshape(FACES, FACE_ROWS, normal_loads)
    gathered = faces.astype(jnp.float32)
    for moved, pack, place, sel_own, unpack in tables:
        outgoing = jnp.einsum(
            "jb,brl->jrl", pack, faces, preferred_element_type=jnp.float32
        ).astype(jnp.bfloat16)
        arrived = passed_along(outgoing, SUB, -moved)
        gathered = gathered + jnp.einsum(
            "fj,jrl->frl", place, arrived, preferred_element_type=jnp.float32
        )
    zfull = jnp.concatenate(
        [gathered.astype(jnp.bfloat16).reshape(face_total, normal_loads), low[face_total:]], axis=0
    )
    image = jnp.dot(dual_ops[0], zfull, preferred_element_type=jnp.float32).astype(jnp.bfloat16)
    yfaces = image[:face_total].reshape(FACES, FACE_ROWS, normal_loads)
    returned = jnp.zeros((FACES, FACE_ROWS, normal_loads), jnp.float32)
    for moved, pack, place, sel_own, unpack in tables:
        leaving = jnp.einsum(
            "fj,frl->jrl", sel_own, yfaces, preferred_element_type=jnp.float32
        ).astype(jnp.bfloat16)
        coming = passed_along(leaving, SUB, moved)
        returned = returned + jnp.einsum(
            "jb,jrl->brl", unpack, coming, preferred_element_type=jnp.float32
        )
    result = image.astype(jnp.float32)
    return jnp.concatenate(
        [result[:face_total] + returned.reshape(face_total, normal_loads), result[face_total:]],
        axis=0,
    )


def coarse_direction(dual_gradient, modes, coarse_inverse):
    normal_loads = dual_gradient.shape[-1]
    width_cols = coarse_inverse.shape[1]
    residual = jnp.dot(
        modes, dual_gradient, precision=lax.Precision.HIGHEST, preferred_element_type=jnp.float32
    )
    group_rows = lax.all_gather(residual, SUB, axis=0, tiled=True)
    group_rows = group_rows.reshape(lax.axis_size(SUB), 1, MODES, normal_loads)
    regrouped = lax.all_to_all(group_rows, "grp", split_axis=0, concat_axis=1, tiled=True)
    columns = regrouped.reshape(width_cols, normal_loads)
    partial_rows = jnp.dot(
        coarse_inverse, columns, precision=lax.Precision.HIGHEST, preferred_element_type=jnp.float32
    )
    own_corr = sum_at_owner(partial_rows, "grp", 0)
    return dual_gradient - jnp.einsum("mr,ml->rl", modes, own_corr, precision=lax.Precision.HIGHEST)


def on_device(
    lam_start, loads, dual_ops, modes, coarse_inverse, face_offset, face_block, face_sign, contact
):
    tables = build_tables(face_offset, face_block, face_sign)
    lam = lam_start
    for step in range(STEPS):
        dual_gradient = apply_dual(lam, dual_ops, tables) - loads
        search_direction = coarse_direction(dual_gradient, modes, coarse_inverse)
        local_slope = jnp.sum(dual_gradient * search_direction, axis=0)
        slope = over_axes(local_slope, SUB_GRP)
        image = apply_dual(search_direction, dual_ops, tables)
        curv = over_axes(jnp.sum(search_direction * image, axis=0), SUB_GRP)
        alpha = slope / curv
        lam = lam - alpha[None, :] * search_direction
        active = contact[step][:, None] == 1
        lam = jnp.where(active, jnp.maximum(lam, 0.0), lam)
    return lam


def solution(mesh):
    finer = Mesh(
        mesh.devices.reshape(8, 8, 2, mesh.shape["grp"]), ("sub_0", "sub_1", "sub_2", "grp")
    )
    placed = (
        P(SUB_GRP, None),
        P(SUB_GRP, None),
        P(SUB_GRP, None, None),
        P(None, SUB_GRP),
        P(SUB, "grp"),
        P(None, "grp", None),
        P(None, "grp", None),
        P(None, "grp", None),
        P(None, SUB_GRP),
    )
    return jax.shard_map(
        on_device, mesh=finer, in_specs=placed, out_specs=P(SUB_GRP, None), check_vma=False
    )
```

profile of v0, /device:TPU:1, one launch (start us, length us, event | category | flops | bytes accessed | tf_op | source)
XLA Modules:
  0.0 694.3 jit_solution(9550296484969539643)
XLA Ops:
  6.0 8.7 %collective-permute-start.2 = (bf16[4,32,128]{2,0,1:T(4,128)(2,1)S(1)}, bf16[4,32,128]{2,0,1:T(4,128)(2,1)S(1)}, u32[]{:S(2)}, u32[]{:S(2)}) collective-permute-start(bf16[4,32,128]{2,0,1:T(4,128)(2,1)S(1)} %convolution_convert_fusion.45), channel_id=1, source_target_pairs={{4,0},{8,4},{12,8},{16,12},{20,16},{24,20},{28,24},{32,28},{36,32}... | collective-permute-start | bytes 98312 | tf_op jit(solution)/shard_map/ppermute | solution.py:19
  44.6 60.7 %all-gather = f32[128,6,128]{2,1,0:T(8,128)S(1)} all-gather(f32[1,6,128]{2,1,0:T(8,128)S(1)} %convolution_bitcast_fusion.8), channel_id=1, replica_groups=mesh['sub_0'=8,'sub_1'=8,'sub_2'=2,'grp'=4] {'sub_0','sub_1','sub_2'}, dimensions={0}, use_global_device_ids=true | all-gather | bytes 396288 | tf_op jit(solution)/shard_map/all_gather | solution.py:114
  105.7 11.5 %all_to_all.60 = f32[128,1,6,128]{3,1,2,0:T(1,128)S(1)} all-to-all(f32[128,1,6,128]{3,1,2,0:T(1,128)S(1)} %copy.93), channel_id=1, replica_groups=mesh['sub_0'=8,'sub_1'=8,'sub_2'=2,'grp'=4] {'grp'}, dimensions={0} | all-to-all | bytes 786432 | tf_op jit(solution)/shard_map/all_to_all | solution.py:116
  188.1 17.3 %all-reduce.5 = (f32[128]{0:T(128)S(1)}, f32[128]{0:T(128)S(1)}) all-reduce(f32[128]{0:T(128)} %get-tuple-element.10, f32[128]{0:T(128)} %get-tuple-element.9), channel_id=1, replica_groups=mesh['sub_0'=8,'sub_1'=8,'sub_2'=2,'grp'=4] {'sub_0'}, use_global_device_ids=true, to_apply=%region_10.11 | all-reduce | flops 256 | bytes 2048 | tf_op jit(solution)/shard_map/psum | solution.py:36
  205.4 14.3 %all-reduce.2 = (f32[128]{0:T(128)S(1)}, f32[128]{0:T(128)S(1)}) all-reduce(f32[128]{0:T(128)S(1)} %get-tuple-element.33, f32[128]{0:T(128)S(1)} %get-tuple-element.34), channel_id=1, replica_groups=mesh['sub_0'=8,'sub_1'=8,'sub_2'=2,'grp'=4] {'sub_1'}, use_global_device_ids=true, to_apply=%region_11.12 | all-reduce | flops 256 | bytes 2048 | tf_op jit(solution)/shard_map/psum | solution.py:36
  219.7 9.8 %all-reduce.11 = (f32[128]{0:T(128)S(1)}, f32[128]{0:T(128)S(1)}) all-reduce(f32[128]{0:T(128)S(1)} %get-tuple-element.27, f32[128]{0:T(128)S(1)} %get-tuple-element.28), channel_id=1, replica_groups=mesh['sub_0'=8,'sub_1'=8,'sub_2'=2,'grp'=4] {'sub_2'}, use_global_device_ids=true, to_apply=%region_12.13 | all-reduce | flops 256 | bytes 2048 | tf_op jit(solution)/shard_map/psum | solution.py:36
  229.5 7.0 %all-reduce.8 = (f32[128]{0:T(128)S(1)}, f32[128]{0:T(128)S(1)}) all-reduce(f32[128]{0:T(128)S(1)} %get-tuple-element.45, f32[128]{0:T(128)S(1)} %get-tuple-element.46), channel_id=1, replica_groups=mesh['sub_0'=8,'sub_1'=8,'sub_2'=2,'grp'=4] {'grp'}, use_global_device_ids=true, to_apply=%region_13.14 | all-reduce | flops 256 | bytes 2048 | tf_op jit(solution)/shard_map/psum | solution.py:36
  240.3 5.8 collective-permute-start.17
  280.8 57.2 %all-gather.1 = f32[128,6,128]{2,1,0:T(8,128)S(1)} all-gather(f32[1,6,128]{2,1,0:T(8,128)S(1)} %convolution_bitcast_fusion.7), channel_id=1, replica_groups=mesh['sub_0'=8,'sub_1'=8,'sub_2'=2,'grp'=4] {'sub_0','sub_1','sub_2'}, dimensions={0}, use_global_device_ids=true | all-gather | bytes 396288 | tf_op jit(solution)/shard_map/all_gather | solution.py:114
  338.4 10.2 %all_to_all.61 = f32[128,1,6,128]{3,1,2,0:T(1,128)S(1)} all-to-all(f32[128,1,6,128]{3,1,2,0:T(1,128)S(1)} %copy.127), channel_id=1, replica_groups=mesh['sub_0'=8,'sub_1'=8,'sub_2'=2,'grp'=4] {'grp'}, dimensions={0} | all-to-all | bytes 786432 | tf_op jit(solution)/shard_map/all_to_all | solution.py:116
  353.9 7.2 %all_to_all.62 = f32[4,6,128]{2,1,0:T(8,128)} all-to-all(f32[4,6,128]{2,1,0:T(8,128)S(1)} %reshape.613), channel_id=1, replica_groups=mesh['sub_0'=8,'sub_1'=8,'sub_2'=2,'grp'=4] {'grp'}, dimensions={0} | all-to-all | bytes 24576 | tf_op jit(solution)/shard_map/all_to_all | solution.py:30
  370.7 6.6 collective-permute-start.25
  424.1 17.2 %all-reduce.4 = (f32[128]{0:T(128)S(1)}, f32[128]{0:T(128)S(1)}) all-reduce(f32[128]{0:T(128)} %get-tuple-element.8, f32[128]{0:T(128)} %get-tuple-element.7), channel_id=1, replica_groups=mesh['sub_0'=8,'sub_1'=8,'sub_2'=2,'grp'=4] {'sub_0'}, use_global_device_ids=true, to_apply=%region_21.22 | all-reduce | flops 256 | bytes 2048 | tf_op jit(solution)/shard_map/psum | solution.py:36
  441.2 14.3 %all-reduce.1 = (f32[128]{0:T(128)S(1)}, f32[128]{0:T(128)S(1)}) all-reduce(f32[128]{0:T(128)S(1)} %get-tuple-element.31, f32[128]{0:T(128)S(1)} %get-tuple-element.32), channel_id=1, replica_groups=mesh['sub_0'=8,'sub_1'=8,'sub_2'=2,'grp'=4] {'sub_1'}, use_global_device_ids=true, to_apply=%region_22.23 | all-reduce | flops 256 | bytes 2048 | tf_op jit(solution)/shard_map/psum | solution.py:36
  455.5 9.8 %all-reduce.10 = (f32[128]{0:T(128)S(1)}, f32[128]{0:T(128)S(1)}) all-reduce(f32[128]{0:T(128)S(1)} %get-tuple-element.25, f32[128]{0:T(128)S(1)} %get-tuple-element.26), channel_id=1, replica_groups=mesh['sub_0'=8,'sub_1'=8,'sub_2'=2,'grp'=4] {'sub_2'}, use_global_device_ids=true, to_apply=%region_23.24 | all-reduce | flops 256 | bytes 2048 | tf_op jit(solution)/shard_map/psum | solution.py:36
  465.3 6.8 all-reduce.7
  508.6 57.4 %all-gather.2 = f32[128,6,128]{2,1,0:T(8,128)S(1)} all-gather(f32[1,6,128]{2,1,0:T(8,128)S(1)} %convolution_bitcast_fusion.6), channel_id=1, replica_groups=mesh['sub_0'=8,'sub_1'=8,'sub_2'=2,'grp'=4] {'sub_0','sub_1','sub_2'}, dimensions={0}, use_global_device_ids=true | all-gather | bytes 396288 | tf_op jit(solution)/shard_map/all_gather | solution.py:114
  566.4 10.2 %all_to_all.63 = f32[128,1,6,128]{3,1,2,0:T(1,128)S(1)} all-to-all(f32[128,1,6,128]{3,1,2,0:T(1,128)S(1)} %copy.160), channel_id=1, replica_groups=mesh['sub_0'=8,'sub_1'=8,'sub_2'=2,'grp'=4] {'grp'}, dimensions={0} | all-to-all | bytes 786432 | tf_op jit(solution)/shard_map/all_to_all | solution.py:116
  578.8 6.6 all_to_all.64
  593.4 6.6 collective-permute-start.41
  644.1 17.1 %all-reduce.3 = (f32[128]{0:T(128)S(1)}, f32[128]{0:T(128)S(1)}) all-reduce(f32[128]{0:T(128)S(1)} %get-tuple-element.6, f32[128]{0:T(128)S(1)} %get-tuple-element.5), channel_id=1, replica_groups=mesh['sub_0'=8,'sub_1'=8,'sub_2'=2,'grp'=4] {'sub_0'}, use_global_device_ids=true, to_apply=%region_32.33 | all-reduce | flops 256 | bytes 2048 | tf_op jit(solution)/shard_map/psum | solution.py:36
  661.2 14.3 %all-reduce = (f32[128]{0:T(128)S(1)}, f32[128]{0:T(128)S(1)}) all-reduce(f32[128]{0:T(128)S(1)} %get-tuple-element.29, f32[128]{0:T(128)S(1)} %get-tuple-element.30), channel_id=1, replica_groups=mesh['sub_0'=8,'sub_1'=8,'sub_2'=2,'grp'=4] {'sub_1'}, use_global_device_ids=true, to_apply=%region_33.34 | all-reduce | flops 256 | bytes 2048 | tf_op jit(solution)/shard_map/psum | solution.py:36
  675.5 9.8 %all-reduce.9 = (f32[128]{0:T(128)S(1)}, f32[128]{0:T(128)S(1)}) all-reduce(f32[128]{0:T(128)S(1)} %get-tuple-element.23, f32[128]{0:T(128)S(1)} %get-tuple-element.24), channel_id=1, replica_groups=mesh['sub_0'=8,'sub_1'=8,'sub_2'=2,'grp'=4] {'sub_2'}, use_global_device_ids=true, to_apply=%region_34.35 | all-reduce | flops 256 | bytes 2048 | tf_op jit(solution)/shard_map/psum | solution.py:36
  685.3 6.8 all-reduce.6
  (472 shorter events, 299.2 us)
Async XLA Ops:
  4.1 22.9 %collective-permute-start.3 = (bf16[4,32,128]{2,0,1:T(4,128)(2,1)S(1)}, bf16[4,32,128]{2,0,1:T(4,128)(2,1)S(1)}, u32[]{:S(2)}, u32[]{:S(2)}) collective-permute-start(bf16[4,32,128]{2,0,1:T(4,128)(2,1)S(1)} %convolution_convert_fusion.44), channel_id=1, source_target_pairs={{8,0},{12,4},{16,8},{20,12},{24,16},{28,20},{32,24},{36,28},{40,32... | collective-permute-start | bytes 98312 | tf_op jit(solution)/shard_map/ppermute | solution.py:19
  6.0 20.8 %collective-permute-start.2 = (bf16[4,32,128]{2,0,1:T(4,128)(2,1)S(1)}, bf16[4,32,128]{2,0,1:T(4,128)(2,1)S(1)}, u32[]{:S(2)}, u32[]{:S(2)}) collective-permute-start(bf16[4,32,128]{2,0,1:T(4,128)(2,1)S(1)} %convolution_convert_fusion.45), channel_id=1, source_target_pairs={{4,0},{8,4},{12,8},{16,12},{20,16},{24,20},{28,24},{32,28},{36,32}... | collective-permute-start | bytes 98312 | tf_op jit(solution)/shard_map/ppermute | solution.py:19
  15.4 11.2 %collective-permute-start.1 = (bf16[4,32,128]{2,0,1:T(4,128)(2,1)S(1)}, bf16[4,32,128]{2,0,1:T(4,128)(2,1)S(1)}, u32[]{:S(2)}, u32[]{:S(2)}) collective-permute-start(bf16[4,32,128]{2,0,1:T(4,128)(2,1)S(1)} %convolution_convert_fusion.46), channel_id=1, source_target_pairs={{0,4},{4,8},{8,12},{12,16},{16,20},{20,24},{24,28},{28,32},{32,36}... | collective-permute-start | bytes 98312 | tf_op jit(solution)/shard_map/ppermute | solution.py:19
  29.7 11.6 %collective-permute-start.5 = (bf16[4,32,128]{2,0,1:T(4,128)(2,1)S(1)}, bf16[4,32,128]{2,0,1:T(4,128)(2,1)S(1)}, u32[]{:S(2)}, u32[]{:S(2)}) collective-permute-start(bf16[4,32,128]{2,0,1:T(4,128)(2,1)S(1)} %convolution_convert_fusion.42), channel_id=1, source_target_pairs={{4,0},{8,4},{12,8},{16,12},{20,16},{24,20},{28,24},{32,28},{36,32}... | collective-permute-start | bytes 98312 | tf_op jit(solution)/shard_map/ppermute | solution.py:19
  32.6 10.2 %collective-permute-start.4 = (bf16[4,32,128]{2,0,1:T(4,128)(2,1)S(1)}, bf16[4,32,128]{2,0,1:T(4,128)(2,1)S(1)}, u32[]{:S(2)}, u32[]{:S(2)}) collective-permute-start(bf16[4,32,128]{2,0,1:T(4,128)(2,1)S(1)} %convolution_convert_fusion.43), channel_id=1, source_target_pairs={{8,0},{12,4},{16,8},{20,12},{24,16},{28,20},{32,24},{36,28},{40,32... | collective-permute-start | bytes 98312 | tf_op jit(solution)/shard_map/ppermute | solution.py:19
  136.5 14.9 %collective-permute-start.9 = (bf16[4,32,128]{2,0,1:T(4,128)(2,1)S(1)}, bf16[4,32,128]{2,0,1:T(4,128)(2,1)S(1)}, u32[]{:S(2)}, u32[]{:S(2)}) collective-permute-start(bf16[4,32,128]{2,0,1:T(4,128)(2,1)S(1)} %convolution_convert_fusion.38), channel_id=1, source_target_pairs={{0,4},{4,8},{8,12},{12,16},{16,20},{20,24},{24,28},{28,32},{32,36}... | collective-permute-start | bytes 98312 | tf_op jit(solution)/shard_map/ppermute | solution.py:19
  164.1 15.3 %collective-permute-start.13 = (bf16[4,32,128]{2,0,1:T(4,128)(2,1)S(1)}, bf16[4,32,128]{2,0,1:T(4,128)(2,1)S(1)}, u32[]{:S(2)}, u32[]{:S(2)}) collective-permute-start(bf16[4,32,128]{2,0,1:T(4,128)(2,1)S(1)} %convolution_convert_fusion.34), channel_id=1, source_target_pairs={{4,0},{8,4},{12,8},{16,12},{20,16},{24,20},{28,24},{32,28},{36,32}... | collective-permute-start | bytes 98312 | tf_op jit(solution)/shard_map/ppermute | solution.py:19
  169.3 12.8 %collective-permute-start.12 = (bf16[4,32,128]{2,0,1:T(4,128)(2,1)S(1)}, bf16[4,32,128]{2,0,1:T(4,128)(2,1)S(1)}, u32[]{:S(2)}, u32[]{:S(2)}) collective-permute-start(bf16[4,32,128]{2,0,1:T(4,128)(2,1)S(1)} %convolution_convert_fusion.35), channel_id=1, source_target_pairs={{8,0},{12,4},{16,8},{20,12},{24,16},{28,20},{32,24},{36,28},{40,32... | collective-permute-start | bytes 98312 | tf_op jit(solution)/shard_map/ppermute | solution.py:19
  170.6 10.6 %collective-permute-start.15 = (bf16[4,32,128]{2,0,1:T(4,128)(2,1)S(1)}, bf16[4,32,128]{2,0,1:T(4,128)(2,1)S(1)}, u32[]{:S(2)}, u32[]{:S(2)}) collective-permute-start(bf16[4,32,128]{2,0,1:T(4,128)(2,1)S(1)} %convolution_convert_fusion.32), channel_id=1, source_target_pairs={{0,8},{4,12},{8,16},{12,20},{16,24},{20,28},{24,32},{28,36},{32,40... | collective-permute-start | bytes 98312 | tf_op jit(solution)/shard_map/ppermute | solution.py:19
  240.3 14.8 %collective-permute-start.17 = (bf16[4,32,128]{2,0,1:T(4,128)(2,1)S(1)}, bf16[4,32,128]{2,0,1:T(4,128)(2,1)S(1)}, u32[]{:S(2)}, u32[]{:S(2)}) collective-permute-start(bf16[4,32,128]{2,0,1:T(4,128)(2,1)S(1)} %convolution_convert_fusion.30), channel_id=1, source_target_pairs={{0,4},{4,8},{8,12},{12,16},{16,20},{20,24},{24,28},{28,32},{32,36}... | collective-permute-start | bytes 98312 | tf_op jit(solution)/shard_map/ppermute | solution.py:19
  260.2 13.7 %collective-permute-start.21 = (bf16[4,32,128]{2,0,1:T(4,128)(2,1)S(1)}, bf16[4,32,128]{2,0,1:T(4,128)(2,1)S(1)}, u32[]{:S(2)}, u32[]{:S(2)}) collective-permute-start(bf16[4,32,128]{2,0,1:T(4,128)(2,1)S(1)} %convolution_convert_fusion.26), channel_id=1, source_target_pairs={{4,0},{8,4},{12,8},{16,12},{20,16},{24,20},{28,24},{32,28},{36,32}... | collective-permute-start | bytes 98312 | tf_op jit(solution)/shard_map/ppermute | solution.py:19
  263.9 11.5 %collective-permute-start.20 = (bf16[4,32,128]{2,0,1:T(4,128)(2,1)S(1)}, bf16[4,32,128]{2,0,1:T(4,128)(2,1)S(1)}, u32[]{:S(2)}, u32[]{:S(2)}) collective-permute-start(bf16[4,32,128]{2,0,1:T(4,128)(2,1)S(1)} %convolution_convert_fusion.27), channel_id=1, source_target_pairs={{8,0},{12,4},{16,8},{20,12},{24,16},{28,20},{32,24},{36,28},{40,32... | collective-permute-start | bytes 98312 | tf_op jit(solution)/shard_map/ppermute | solution.py:19
  265.2 10.0 %collective-permute-start.23 = (bf16[4,32,128]{2,0,1:T(4,128)(2,1)S(1)}, bf16[4,32,128]{2,0,1:T(4,128)(2,1)S(1)}, u32[]{:S(2)}, u32[]{:S(2)}) collective-permute-start(bf16[4,32,128]{2,0,1:T(4,128)(2,1)S(1)} %convolution_convert_fusion.24), channel_id=1, source_target_pairs={{0,8},{4,12},{8,16},{12,20},{16,24},{20,28},{24,32},{28,36},{32,40... | collective-permute-start | bytes 98312 | tf_op jit(solution)/shard_map/ppermute | solution.py:19
  370.7 16.5 %collective-permute-start.25 = (bf16[4,32,128]{2,0,1:T(4,128)(2,1)S(1)}, bf16[4,32,128]{2,0,1:T(4,128)(2,1)S(1)}, u32[]{:S(2)}, u32[]{:S(2)}) collective-permute-start(bf16[4,32,128]{2,0,1:T(4,128)(2,1)S(1)} %convolution_convert_fusion.22), channel_id=1, source_target_pairs={{0,4},{4,8},{8,12},{12,16},{16,20},{20,24},{24,28},{28,32},{32,36}... | collective-permute-start | bytes 98312 | tf_op jit(solution)/shard_map/ppermute | solution.py:19
  399.9 15.3 %collective-permute-start.29 = (bf16[4,32,128]{2,0,1:T(4,128)(2,1)S(1)}, bf16[4,32,128]{2,0,1:T(4,128)(2,1)S(1)}, u32[]{:S(2)}, u32[]{:S(2)}) collective-permute-start(bf16[4,32,128]{2,0,1:T(4,128)(2,1)S(1)} %convolution_convert_fusion.18), channel_id=1, source_target_pairs={{4,0},{8,4},{12,8},{16,12},{20,16},{24,20},{28,24},{32,28},{36,32}... | collective-permute-start | bytes 98312 | tf_op jit(solution)/shard_map/ppermute | solution.py:19
  405.1 12.8 %collective-permute-start.28 = (bf16[4,32,128]{2,0,1:T(4,128)(2,1)S(1)}, bf16[4,32,128]{2,0,1:T(4,128)(2,1)S(1)}, u32[]{:S(2)}, u32[]{:S(2)}) collective-permute-start(bf16[4,32,128]{2,0,1:T(4,128)(2,1)S(1)} %convolution_convert_fusion.19), channel_id=1, source_target_pairs={{8,0},{12,4},{16,8},{20,12},{24,16},{28,20},{32,24},{36,28},{40,32... | collective-permute-start | bytes 98312 | tf_op jit(solution)/shard_map/ppermute | solution.py:19
  406.4 10.6 %collective-permute-start.31 = (bf16[4,32,128]{2,0,1:T(4,128)(2,1)S(1)}, bf16[4,32,128]{2,0,1:T(4,128)(2,1)S(1)}, u32[]{:S(2)}, u32[]{:S(2)}) collective-permute-start(bf16[4,32,128]{2,0,1:T(4,128)(2,1)S(1)} %convolution_convert_fusion.16), channel_id=1, source_target_pairs={{0,8},{4,12},{8,16},{12,20},{16,24},{20,28},{24,32},{28,36},{32,40... | collective-permute-start | bytes 98312 | tf_op jit(solution)/shard_map/ppermute | solution.py:19
  475.0 13.3 %collective-permute-start.33 = (bf16[4,32,128]{2,0,1:T(4,128)(2,1)S(1)}, bf16[4,32,128]{2,0,1:T(4,128)(2,1)S(1)}, u32[]{:S(2)}, u32[]{:S(2)}) collective-permute-start(bf16[4,32,128]{2,0,1:T(4,128)(2,1)S(1)} %convolution_convert_fusion.14), channel_id=1, source_target_pairs={{0,4},{4,8},{8,12},{12,16},{16,20},{20,24},{24,28},{28,32},{32,36}... | collective-permute-start | bytes 98312 | tf_op jit(solution)/shard_map/ppermute | solution.py:19
  491.9 12.8 %collective-permute-start.37 = (bf16[4,32,128]{2,0,1:T(4,128)(2,1)S(1)}, bf16[4,32,128]{2,0,1:T(4,128)(2,1)S(1)}, u32[]{:S(2)}, u32[]{:S(2)}) collective-permute-start(bf16[4,32,128]{2,0,1:T(4,128)(2,1)S(1)} %convolution_convert_fusion.10), channel_id=1, source_target_pairs={{4,0},{8,4},{12,8},{16,12},{20,16},{24,20},{28,24},{32,28},{36,32}... | collective-permute-start | bytes 98312 | tf_op jit(solution)/shard_map/ppermute | solution.py:19
  494.7 11.5 %collective-permute-start.36 = (bf16[4,32,128]{2,0,1:T(4,128)(2,1)S(1)}, bf16[4,32,128]{2,0,1:T(4,128)(2,1)S(1)}, u32[]{:S(2)}, u32[]{:S(2)}) collective-permute-start(bf16[4,32,128]{2,0,1:T(4,128)(2,1)S(1)} %convolution_convert_fusion.11), channel_id=1, source_target_pairs={{8,0},{12,4},{16,8},{20,12},{24,16},{28,20},{32,24},{36,28},{40,32... | collective-permute-start | bytes 98312 | tf_op jit(solution)/shard_map/ppermute | solution.py:19
  496.0 10.0 %collective-permute-start.39 = (bf16[4,32,128]{2,0,1:T(4,128)(2,1)S(1)}, bf16[4,32,128]{2,0,1:T(4,128)(2,1)S(1)}, u32[]{:S(2)}, u32[]{:S(2)}) collective-permute-start(bf16[4,32,128]{2,0,1:T(4,128)(2,1)S(1)} %convolution_convert_fusion.8), channel_id=1, source_target_pairs={{0,8},{4,12},{8,16},{12,20},{16,24},{20,28},{24,32},{28,36},{32,40... | collective-permute-start | bytes 98312 | tf_op jit(solution)/shard_map/ppermute | solution.py:19
  593.4 16.5 %collective-permute-start.41 = (bf16[4,32,128]{2,0,1:T(4,128)(2,1)S(1)}, bf16[4,32,128]{2,0,1:T(4,128)(2,1)S(1)}, u32[]{:S(2)}, u32[]{:S(2)}) collective-permute-start(bf16[4,32,128]{2,0,1:T(4,128)(2,1)S(1)} %convolution_convert_fusion.6), channel_id=1, source_target_pairs={{0,4},{4,8},{8,12},{12,16},{16,20},{20,24},{24,28},{28,32},{32,36}... | collective-permute-start | bytes 98312 | tf_op jit(solution)/shard_map/ppermute | solution.py:19
  622.6 15.3 %collective-permute-start.45 = (bf16[4,32,128]{2,0,1:T(4,128)(2,1)S(1)}, bf16[4,32,128]{2,0,1:T(4,128)(2,1)S(1)}, u32[]{:S(2)}, u32[]{:S(2)}) collective-permute-start(bf16[4,32,128]{2,0,1:T(4,128)(2,1)S(1)} %convolution_convert_fusion.2), channel_id=1, source_target_pairs={{4,0},{8,4},{12,8},{16,12},{20,16},{24,20},{28,24},{32,28},{36,32}... | collective-permute-start | bytes 98312 | tf_op jit(solution)/shard_map/ppermute | solution.py:19
  627.8 11.5 %collective-permute-start.44 = (bf16[4,32,128]{2,0,1:T(4,128)(2,1)S(1)}, bf16[4,32,128]{2,0,1:T(4,128)(2,1)S(1)}, u32[]{:S(2)}, u32[]{:S(2)}) collective-permute-start(bf16[4,32,128]{2,0,1:T(4,128)(2,1)S(1)} %convolution_convert_fusion.3), channel_id=1, source_target_pairs={{8,0},{12,4},{16,8},{20,12},{24,16},{28,20},{32,24},{36,28},{40,32... | collective-permute-start | bytes 98312 | tf_op jit(solution)/shard_map/ppermute | solution.py:19
  (95 other events, 2096.4 us)
where the time goes:
time: 700 us; the launch traced here: 694 us
  blocking collectives  366 us (52%)
  starting transfers between devices  160 us (23%)
  matrix products  75.2 us (11%)
  local copies, waits for them, and re-layouts  61.6 us (9%)
  other arithmetic  25 us (4%)
    all_gather x3, blocking collectives, coarse_direction(): group_rows = lax.all_gather(residual, SUB, axis=0, tiled=True)  175 us
    ppermute x48, starting transfers between devices, passed_along(): lax.ppermute(value, axis, [(source, source + steps) for source in range(l...  157 us
    psum x12, blocking collectives, over_axes(): x = lax.psum(x, axis)  145 us
    all_to_all x3, blocking collectives, coarse_direction(): lax.all_to_all(group_rows, 'grp', split_axis=0, concat_axis=1, tiled=True)  32 us
    dot_general x24, matrix products, apply_dual(): jnp.einsum('jb,brl->jrl', pack, faces, preferred_element_type=jnp.float32)  16.3 us
  transfers between devices with their start and end apart: 49, of which 12 were waited for; matrix products, arithmetic and copies ran while one was open for 6% of the time, Pallas kernels for 0%

commit v1 on v0

v1 whole, which is shorter than its diff:
```python
import jax
import jax.numpy as jnp
from jax import lax
from jax.experimental import pallas as pl
from jax.experimental.pallas import tpu as pltpu
from jax.sharding import PartitionSpec as P

MESH = pl.DeviceIdType.MESH
FACES = 8
FACE_ROWS = 32
FACE_TOTAL = FACES * FACE_ROWS
CAP = 4
SLOTS = 4 * CAP
MODES = 6
STEPS = 3
MOVES = (-2, -1, 1, 2)
NY, NL, NX = 8, 16, 4
NXY = NY * NX
ORDER = 1024
LOADS = 128
F32, BF16 = jnp.float32, jnp.bfloat16
LOW = -3.0e38


def dot(a, b):
    return jnp.dot(a, b, preferred_element_type=F32)


def dot_t(a, b):
    return lax.dot_general(a, b, (((0,), (0,)), ((), ())), preferred_element_type=F32)


def parts_of(x, count):
    parts = []
    for _ in range(count):
        part = x.astype(BF16).astype(F32)
        parts.append(part)
        x = x - part
    return parts


def wait_bytes(sem, ref):
    pltpu.make_async_copy(ref, ref, sem).wait()


def kernel(face_offset, face_block, face_sign, lam_in, loads, dual, modes, cinv, contact, out, *scratch):
    (place, leave, pick, vz, ybf, zf, grad, dirn, modes_rows, modes_cols, floor, spread, fsend, bsend, eline, part, cpl, arl, arp,
     csend, cmat, cpad, fs, fr, bs, br, es, er, cs, cr, als, alr, aps, apr, ks, kr) = scratch[:36]
    farr = scratch[36:42]
    barr = scratch[42:45]
    s = lax.axis_index("sub")
    x = lax.axis_index("grp")
    n_sub = NY * NL
    y = s // NL
    l = s % NL
    me = y * NX + x

    barrier = pltpu.get_barrier_semaphore()

    def line_dev(i):
        return (y * NL + (l + i) % NL, x)

    def plane_idx(i):
        return (me + i) % NXY

    def plane_dev(q):
        return ((q // NX) * NL + l, q % NX)

    def around(move):
        return ((s + move + n_sub) % n_sub, x)

    def greet(device):
        pl.semaphore_signal(barrier, 1, device_id=device, device_id_type=MESH)

    def greet_line(i, carry):
        greet(line_dev(i))
        return carry

    def greet_plane(i, carry):
        greet(plane_dev(plane_idx(i)))
        return carry

    for move in MOVES:
        greet(around(move))
    lax.fori_loop(1, NL, greet_line, 0)
    lax.fori_loop(1, NXY, greet_plane, 0)

    def remote(src, dst, ssem, rsem, device):
        pltpu.make_async_remote_copy(
            src_ref=src, dst_ref=dst, send_sem=ssem, recv_sem=rsem, device_id=device, device_id_type=MESH
        ).start()

    def same_row(rows, cols):
        row = lax.broadcasted_iota(jnp.int32, (rows, cols), 0)
        col = lax.broadcasted_iota(jnp.int32, (rows, cols), 1)
        return jnp.where(row % FACE_ROWS == col % FACE_ROWS, col // FACE_ROWS, -1)

    wide = same_row(FACE_ROWS, SLOTS * FACE_ROWS)
    narrow = same_row(FACE_ROWS, FACE_TOTAL)
    own_off = [face_offset[f, s] for f in range(FACES)]
    own_slot = []
    for f in range(FACES):
        rank = jnp.int32(0)
        for g in range(f):
            rank = rank + jnp.where(own_off[g] == own_off[f], 1, 0)
        own_slot.append(own_off[f] * CAP + rank)
        sign = (2 * face_sign[f, s] - 1).astype(F32)
        place[f * FACE_ROWS : (f + 1) * FACE_ROWS, :] = jnp.where(wide == own_slot[f], sign, 0.0).astype(BF16)
    for q in range(SLOTS):
        face = jnp.int32(0)
        for f in range(FACES):
            face = face + jnp.where(own_slot[f] == q, f, 0)
        leave[q * FACE_ROWS : (q + 1) * FACE_ROWS, :] = jnp.where(narrow == face, 1.0, 0.0).astype(BF16)
    lane = lax.broadcasted_iota(jnp.int32, (1, SLOTS * FACE_ROWS), 1)
    block_of = jnp.full((1, SLOTS * FACE_ROWS), -1, jnp.int32)
    sign_of = jnp.zeros((1, SLOTS * FACE_ROWS), F32)
    for w, move in enumerate(MOVES):
        reader = (s - move + n_sub) % n_sub
        far_off = [face_offset[f, reader] for f in range(FACES)]
        far_block = [face_block[f, reader] for f in range(FACES)]
        far_sign = [2 * face_sign[f, reader] - 1 for f in range(FACES)]
        count = jnp.int32(0)
        slot_of = []
        for f in range(FACES):
            hit = far_off[f] == w
            slot_of.append(jnp.where(hit, count, -1))
            count = count + jnp.where(hit, 1, 0)
        for j in range(CAP):
            q = w * CAP + j
            block = jnp.int32(0)
            sign = jnp.int32(0)
            for f in range(FACES):
                hit = slot_of[f] == j
                block = block + jnp.where(hit, far_block[f], 0)
                sign = sign + jnp.where(hit, far_sign[f], 0)
            pick[q * FACE_ROWS : (q + 1) * FACE_ROWS, :] = jnp.where(narrow == block, 1.0, 0.0).astype(BF16)
            inside = lane // FACE_ROWS == q
            block_of = jnp.where(inside, block, block_of)
            sign_of = jnp.where(inside, sign.astype(F32), sign_of)
    for b in range(FACES):
        hit = (wide >= 0) & (block_of == b)
        spread[b * FACE_ROWS : (b + 1) * FACE_ROWS, :] = jnp.where(hit, sign_of, 0.0).astype(BF16)

    def pack_and_send(n):
        packed = dot(pick[...], vz[0:FACE_TOTAL, :]).astype(BF16)
        fsend[n] = packed.reshape(SLOTS, FACE_ROWS, LOADS)
        for w, move in enumerate(MOVES):
            span = pl.ds(w * CAP, CAP)
            remote(fsend.at[n, span], farr[n].at[span], fs.at[n], fr.at[n], around(-move))

    out[...] = lam_in[...]
    vz[...] = lam_in[...].astype(BF16)

    pl.semaphore_wait(barrier, len(MOVES) + NL - 1 + NXY - 1)
    pack_and_send(0)

    cpad[...] = jnp.zeros(cpad.shape, F32)
    for b in range(NX):
        cpad[b * 8 : b * 8 + MODES, :] = cinv[b * MODES : (b + 1) * MODES, :]
    half = cinv.shape[1] // 2
    pick_r = lax.broadcasted_iota(jnp.int32, (half, LOADS), 0)
    pick_c = lax.broadcasted_iota(jnp.int32, (half, LOADS), 1)
    stack = jnp.concatenate(parts_of(cpad[...], 3), axis=0).astype(BF16)
    for xd in range(NX):
        want = ((pick_c // 8) * NX + xd) * MODES + pick_c % 8
        choose = jnp.where((pick_r == want) & (pick_c % 8 < MODES), 1.0, 0.0).astype(BF16)
        for h in range(2):
            got = dot(stack[:, h * half : (h + 1) * half], choose)
            csend[xd * 2 + h] = got[0:32] + got[32:64] + got[64:96]
    for xd in range(NX):
        for h in range(2):
            yd = 2 * x + h
            mine = (yd == y) & (x == xd)

            @pl.when(mine)
            def _():
                pltpu.make_async_copy(csend.at[xd * 2 + h], cmat.at[y], kr).start()

            @pl.when(jnp.logical_not(mine))
            def _():
                remote(csend.at[xd * 2 + h], cmat.at[y], ks, kr, (yd * NL + l, xd))

    m_pad = jnp.concatenate([modes[...], jnp.zeros((2, ORDER), F32)], axis=0)
    m_hi, m_lo = parts_of(m_pad, 2)
    modes_rows[...] = jnp.concatenate([m_hi, m_lo], axis=0).astype(BF16)
    m_all = jnp.concatenate([m_hi, m_hi, m_lo, jnp.zeros((8, ORDER), F32)], axis=0).astype(BF16)
    eye = (lax.broadcasted_iota(jnp.int32, (32, 32), 0) == lax.broadcasted_iota(jnp.int32, (32, 32), 1))
    modes_cols[...] = dot_t(m_all, eye.astype(F32).astype(BF16)).astype(BF16)
    con = jnp.concatenate([contact[...].astype(F32), jnp.zeros((16 - STEPS, ORDER), F32)], axis=0).astype(BF16)
    for t in range(STEPS):
        pick_t = (lax.broadcasted_iota(jnp.int32, (16, LOADS), 0) == t).astype(F32).astype(BF16)
        floor[t] = jnp.where(dot_t(con, pick_t) > 0.5, 0.0, LOW)

    def receive_faces(n, keep):
        wait_bytes(fr.at[n], farr[n])
        came = dot(place[...], farr[n][...].reshape(SLOTS * FACE_ROWS, LOADS))
        z = vz[0:FACE_TOTAL, :].astype(F32) + came
        if keep:
            zf[...] = z
        vz[0:FACE_TOTAL, :] = z.astype(BF16)

    def residual(rows_from, rows_to):
        g_hi, g_lo = parts_of(grad[rows_from:rows_to, :], 2)
        m = modes_rows[:, rows_from:rows_to]
        a = dot(m, g_hi.astype(BF16))
        b = dot(m, g_lo.astype(BF16))
        return a[0:8] + a[8:16] + b[0:8]

    for t in range(STEPS):
        if t > 0:
            vz[...] = out[...].astype(BF16)
            pack_and_send(2 * t)
        receive_faces(2 * t, False)
        ybf[...] = dot(dual[0, 0:FACE_TOTAL, :], vz[...]).astype(BF16)
        bsend[t] = dot(leave[...], ybf[...]).astype(BF16).reshape(SLOTS, FACE_ROWS, LOADS)
        for w, move in enumerate(MOVES):
            span = pl.ds(w * CAP, CAP)
            remote(bsend.at[t, span], barr[t].at[span], bs.at[t], br.at[t], around(move))
        y_rest = dot(dual[0, FACE_TOTAL:, :], vz[...]).astype(BF16).astype(F32)
        grad[FACE_TOTAL:, :] = y_rest - loads[FACE_TOTAL:, :]
        e_rest = residual(FACE_TOTAL, ORDER)
        wait_bytes(br.at[t], barr[t])
        back = dot(spread[...], barr[t][...].reshape(SLOTS * FACE_ROWS, LOADS))
        grad[0:FACE_TOTAL, :] = ybf[...].astype(F32) + back - loads[0:FACE_TOTAL, :]
        eline[t, l] = e_rest + residual(0, FACE_TOTAL)

        def send_e(i, carry):
            remote(eline.at[t, l], eline.at[t, l], es.at[t], er.at[t], line_dev(i))
            return carry

        lax.fori_loop(1, NL, send_e, 0)
        if t == 0:
            wait_bytes(kr, cmat)
        wait_bytes(er.at[t], eline.at[t, pl.ds(0, NL - 1)])
        product = jnp.dot(
            cmat[...].reshape(NXY * 8, LOADS), eline[t].reshape(NL * 8, LOADS),
            precision=lax.Precision.HIGHEST, preferred_element_type=F32,
        )
        part[t] = product.reshape(NXY, 8, LOADS)
        cpl[t, me] = part[t, me]

        def send_c(i, carry):
            q = plane_idx(i)
            remote(part.at[t, q], cpl.at[t, me], cs.at[t], cr.at[t], plane_dev(q))
            return carry

        lax.fori_loop(1, NXY, send_c, 0)
        wait_bytes(cr.at[t], cpl.at[t, pl.ds(0, NXY - 1)])
        c_hi, c_lo = parts_of(jnp.sum(cpl[t], axis=0), 2)
        c_all = jnp.concatenate([c_hi, c_lo, c_hi, jnp.zeros((8, LOADS), F32)], axis=0).astype(BF16)
        direction = grad[...] - dot(modes_cols[...], c_all)
        dirn[...] = direction
        vz[...] = direction.astype(BF16)
        pack_and_send(2 * t + 1)
        slope = jnp.sum(grad[...] * direction, axis=0, keepdims=True)

        receive_faces(2 * t + 1, True)
        image = dot(dual[0], vz[...]).astype(BF16).astype(F32)
        curv = jnp.sum(zf[...] * image[0:FACE_TOTAL], axis=0, keepdims=True)
        curv = curv + jnp.sum(dirn[FACE_TOTAL:, :] * image[FACE_TOTAL:], axis=0, keepdims=True)
        arl[t, l] = jnp.concatenate([slope, curv], axis=0)

        def send_line(i, carry):
            remote(arl.at[t, l], arl.at[t, l], als.at[t], alr.at[t], line_dev(i))
            return carry

        lax.fori_loop(1, NL, send_line, 0)
        wait_bytes(alr.at[t], arl.at[t, pl.ds(0, NL - 1)])
        arp[t, me] = jnp.sum(arl[t], axis=0)

        def send_plane(i, carry):
            remote(arp.at[t, me], arp.at[t, me], aps.at[t], apr.at[t], plane_dev(plane_idx(i)))
            return carry

        lax.fori_loop(1, NXY, send_plane, 0)
        wait_bytes(apr.at[t], arp.at[t, pl.ds(0, NXY - 1)])
        total = jnp.sum(arp[t], axis=0)
        alpha = total[0:1] / total[1:2]
        out[...] = jnp.maximum(out[...] - alpha * dirn[...], floor[t])

    for t in range(STEPS):
        for n in (2 * t, 2 * t + 1):
            wait_bytes(fs.at[n], fsend.at[n])
        wait_bytes(bs.at[t], bsend.at[t])
        wait_bytes(es.at[t], eline.at[t, pl.ds(0, NL - 1)])
        wait_bytes(cs.at[t], part.at[t, pl.ds(0, NXY - 1)])
        wait_bytes(als.at[t], arl.at[t, pl.ds(0, NL - 1)])
        wait_bytes(aps.at[t], arp.at[t, pl.ds(0, NXY - 1)])
    own_cut = (x == y // 2)

    @pl.when(own_cut)
    def _():
        wait_bytes(ks, csend.at[pl.ds(0, 7)])

    @pl.when(jnp.logical_not(own_cut))
    def _():
        wait_bytes(ks, csend)


def on_device(lam_start, loads, dual_ops, modes, coarse_inverse, face_offset, face_block, face_sign, contact):
    tables = [face[:, 0, :].T for face in (face_offset, face_block, face_sign)]
    vmem = pl.BlockSpec(memory_space=pltpu.VMEM)
    smem = pl.BlockSpec(memory_space=pltpu.SMEM)
    dma = pltpu.SemaphoreType.DMA
    face_buf = pltpu.VMEM((SLOTS, FACE_ROWS, LOADS), BF16)
    return pl.pallas_call(
        kernel,
        name="dual_steps",
        out_shape=jax.ShapeDtypeStruct(lam_start.shape, F32),
        in_specs=[smem] * 3 + [vmem] * 6,
        out_specs=vmem,
        scratch_shapes=[
            pltpu.VMEM((FACE_TOTAL, SLOTS * FACE_ROWS), BF16),
            pltpu.VMEM((SLOTS * FACE_ROWS, FACE_TOTAL), BF16),
            pltpu.VMEM((SLOTS * FACE_ROWS, FACE_TOTAL), BF16),
            pltpu.VMEM((ORDER, LOADS), BF16),
            pltpu.VMEM((FACE_TOTAL, LOADS), BF16),
            pltpu.VMEM((FACE_TOTAL, LOADS), F32),
            pltpu.VMEM((ORDER, LOADS), F32),
            pltpu.VMEM((ORDER, LOADS), F32),
            pltpu.VMEM((16, ORDER), BF16),
            pltpu.VMEM((ORDER, 32), BF16),
            pltpu.VMEM((STEPS, ORDER, LOADS), F32),
            pltpu.VMEM((FACE_TOTAL, SLOTS * FACE_ROWS), BF16),
            pltpu.VMEM((2 * STEPS, SLOTS, FACE_ROWS, LOADS), BF16),
            pltpu.VMEM((STEPS, SLOTS, FACE_ROWS, LOADS), BF16),
            pltpu.VMEM((STEPS, NL, 8, LOADS), F32),
            pltpu.VMEM((STEPS, NXY, 8, LOADS), F32),
            pltpu.VMEM((STEPS, NXY, 8, LOADS), F32),
            pltpu.VMEM((STEPS, NL, 2, LOADS), F32),
            pltpu.VMEM((STEPS, NXY, 2, LOADS), F32),
            pltpu.VMEM((8, 32, LOADS), F32),
            pltpu.VMEM((8, 32, LOADS), F32),
            pltpu.VMEM((32, coarse_inverse.shape[1]), F32),
            dma((2 * STEPS,)),
            dma((2 * STEPS,)),
        ]
        + [dma((STEPS,))] * 10
        + [dma, dma]
        + [face_buf] * (3 * STEPS),
        compiler_params=pltpu.CompilerParams(collective_id=1, has_side_effects=True),
    )(*tables, lam_start, loads, dual_ops, modes, coarse_inverse, contact)


def solution(mesh):
    both = ("sub", "grp")
    placed = (
        P(both, None),
        P(both, None),
        P(both, None, None),
        P(None, both),
        P("sub", "grp"),
        P(None, "grp", None),
        P(None, "grp", None),
        P(None, "grp", None),
        P(None, both),
    )
    return jax.shard_map(on_device, mesh=mesh, in_specs=placed, out_specs=P(both, None), check_vma=False)
```

time: 700 us -> 143 us (0.20)
  blocking collectives: 366 us -> 0 us
  starting transfers between devices: 160 us -> 0 us
  Pallas kernels: 0 us -> 141 us
  matrix products: 75.2 us -> 0 us
  local copies, waits for them, and re-layouts: 61.6 us -> 1.87 us
  other arithmetic: 25 us -> 0 us
    all_gather x3 -> x0, blocking collectives: 175 us -> none  [coarse_direction(): group_rows = lax.all_gather(residual, SUB, axis=0, tiled=True)]
    ppermute x48 -> x0, starting transfers between devices: 157 us -> none  [passed_along(): lax.ppermute(value, axis, [(source, source + steps) for source in range(l...]
    psum x12 -> x0, blocking collectives: 145 us -> none  [over_axes(): x = lax.psum(x, axis)]
    pallas_call x0 -> x1, Pallas kernels: none -> 141 us  [on_device(): pl.pallas_call(kernel, name='dual_steps', out_shape=jax.ShapeDtypeStruct(...]
    dot_general x119 -> x0, matrix products: 75.2 us -> none  [the longest x24 16.3 us: apply_dual(): jnp.einsum('jb,brl->jrl', pack, faces, preferred_element_type=jnp.float32)]
    all_to_all x5 -> x0, blocking collectives: 45.8 us -> none  [the longest x3 32 us: coarse_direction(): lax.all_to_all(group_rows, 'grp', split_axis=0, concat_axis=1, tiled=True)]
    slice x35 -> x0, local copies, waits for them, and re-layouts: 25.5 us -> none  [the longest x12 6.92 us: apply_dual(): yfaces = image[:face_total].reshape(FACES, FACE_ROWS, normal_loads)]
    reshape x20 -> x0, local copies, waits for them, and re-layouts: 18 us -> none  [the longest x6 6.83 us: apply_dual(): returned.reshape(face_total, normal_loads)]
  transfers between devices with their start and end apart: 49 -> 0, of which waited for: 12 -> 0; matrix products, arithmetic and copies ran while one was open for 6% -> 0% of each run, Pallas kernels for 0% -> 0%
where the time goes in v1:
time: 143 us
  Pallas kernels  141 us (99%)
  local copies, waits for them, and re-layouts  1.87 us (1%)
    pallas_call x1, Pallas kernels, on_device(): pl.pallas_call(kernel, name='dual_steps', out_shape=jax.ShapeDtypeStruct(...  141 us

profile of v1, /device:TPU:1, one launch (start us, length us, event | category | flops | bytes accessed | tf_op | source)
XLA Modules:
  0.0 142.7 jit_solution(15495706088185343325)
XLA Ops:
  0.0 140.9 %dual_steps.1 = f32[1024,128]{1,0:T(8,128)} custom-call(s32[8,128]{1,0:T(8,128)} %bitcast.9, s32[8,128]{1,0:T(8,128)} %bitcast.10, s32[8,128]{1,0:T(8,128)} %bitcast.11, f32[1024,128]{1,0:T(8,128)} %lam_in.1, f32[1024,128]{1,0:T(8,128)} %loads.1, bf16[1,1024,1024]{2,1,0:T(8,128)(2,1)} %dual.1, f32[6,1024]{1,0:T(8,128)} %modes.1, f32[24,768]{1,0:T(8,128)} %cinv.1, ...), custom_call_target="tpu_custom_call" | custom-call | tf_op jit(solution)/shard_map/dual_steps/pallas_call | solution.py:306
  140.9 1.9 %copy.11 = f32[1024,128]{1,0:T(8,128)} copy(f32[1024,128]{1,0:T(8,128)} %dual_steps.1) | data formatting | bytes 1048576

commit v2 on v1

v2 whole, which is shorter than its diff:
```python
import jax
import jax.numpy as jnp
from jax import lax
from jax.experimental import pallas as pl
from jax.experimental.pallas import tpu as pltpu
from jax.sharding import PartitionSpec as P

MESH = pl.DeviceIdType.MESH
FACES = 8
FACE_ROWS = 32
FACE_TOTAL = FACES * FACE_ROWS
CAP = 4
SLOTS = 4 * CAP
SLOT_ROWS = SLOTS * FACE_ROWS
MODES = 6
STEPS = 3
MOVES = (-2, -1, 1, 2)
NY, NL, NX = 8, 16, 4
N_SUB = NY * NL
NXY = NY * NX
ORDER = 1024
LOADS = 128
F32, BF16 = jnp.float32, jnp.bfloat16
LOW = -3.0e38
LAM_HI, LAM_LO, CONTACT, DIR_HI, DIR_LO, MESSAGES = 0, 1, 2, 3, 6, 8


def dot(a, b):
    return jnp.dot(a, b, preferred_element_type=F32)


def dot_t(a, b):
    return lax.dot_general(a, b, (((0,), (0,)), ((), ())), preferred_element_type=F32)


def parts_of(x, count):
    parts = []
    for _ in range(count):
        part = x.astype(BF16).astype(F32)
        parts.append(part)
        x = x - part
    return parts


def iota(shape, dim):
    return lax.broadcasted_iota(jnp.int32, shape, dim)


def ones_where(mask):
    return jnp.where(mask, 1.0, 0.0).astype(BF16)


def same_row(cols):
    row, col = iota((FACE_ROWS, cols), 0), iota((FACE_ROWS, cols), 1)
    return jnp.where(row == (col & (FACE_ROWS - 1)), col >> 5, -1)


def wait_bytes(sem, ref):
    pltpu.make_async_copy(ref, ref, sem).wait()


def ring(step, size):
    return min(step, size - step)


def wrapped(base, step, size):
    return jnp.where(base + step >= size, base + step - size, base + step)


def kernel(face_offset, face_block, face_sign, lam_hbm, loads_hbm, dual_hbm, modes_hbm, cinv_hbm, contact_hbm, out, *scratch):
    (loads, dual, modes, cinv, contact, place, leave, pick, spread, vz, low, ybf, zf, grad, dirn, image, lam_far, modes_rows,
     modes_cols, columns, floor, floor_far, fsend, farr, bsend, barr, eline, part, cpl, arl, arp, csend, cmat, cpad,
     load_sem, fs, fr, bs, br, es, er, cs, cr, als, alr, aps, apr, ks, kr) = scratch
    s = lax.axis_index("sub")
    x = lax.axis_index("grp")
    y = s // NL
    l = s % NL
    me = y * NX + x

    fetches = []
    for i, (src, dst) in enumerate(((lam_hbm, out), (modes_hbm, modes), (cinv_hbm, cinv), (contact_hbm, contact),
                                    (dual_hbm, dual), (loads_hbm, loads))):
        fetches.append(pltpu.make_async_copy(src, dst, load_sem.at[i]))
        fetches[i].start()

    line = [(y * NL + wrapped(l, i, NL), x) for i in sorted(range(1, NL), key=lambda i: -ring(i, NL))]
    ys = [y] + [wrapped(y, i, NY) for i in range(1, NY)]
    xs = [x] + [wrapped(x, i, NX) for i in range(1, NX)]
    steps = sorted(((i, j) for i in range(NY) for j in range(NX) if i + j > 0), key=lambda p: -ring(p[0], NY) - ring(p[1], NX))
    plane = [(ys[i] * NX + xs[j], (ys[i] * NL + l, xs[j])) for i, j in steps]
    around = {move: (wrapped(s, (move + N_SUB) % N_SUB, N_SUB), x) for move in MOVES}

    barrier = pltpu.get_barrier_semaphore()
    for device in [around[move] for move in MOVES] + line + [device for _, device in plane]:
        pl.semaphore_signal(barrier, 1, device_id=device, device_id_type=MESH)

    def remote(src, dst, ssem, rsem, device):
        pltpu.make_async_remote_copy(
            src_ref=src, dst_ref=dst, send_sem=ssem, recv_sem=rsem, device_id=device, device_id_type=MESH
        ).start()

    wide = same_row(SLOT_ROWS)
    narrow = same_row(FACE_TOTAL)
    lane_slot = iota((1, SLOT_ROWS), 1) >> 5
    block_of = jnp.full((1, SLOT_ROWS), -1, jnp.int32)
    sign_of = jnp.zeros((1, SLOT_ROWS), F32)
    for w, move in enumerate(MOVES):
        reader = around[-move][0]
        far_block = [face_block[f, reader] for f in range(FACES)]
        far_sign = [2 * face_sign[f, reader] - 1 for f in range(FACES)]
        count = jnp.int32(0)
        slot_of = []
        for f in range(FACES):
            hit = face_offset[f, reader] == w
            slot_of.append(jnp.where(hit, count, -1))
            count = count + jnp.where(hit, 1, 0)
        for j in range(CAP):
            q = w * CAP + j
            block = jnp.int32(0)
            sign = jnp.int32(0)
            for f in range(FACES):
                hit = slot_of[f] == j
                block = block + jnp.where(hit, far_block[f], 0)
                sign = sign + jnp.where(hit, far_sign[f], 0)
            pick[q * FACE_ROWS : (q + 1) * FACE_ROWS, :] = ones_where(narrow == block)
            block_of = jnp.where(lane_slot == q, block, block_of)
            sign_of = jnp.where(lane_slot == q, sign.astype(F32), sign_of)

    def pack(n, faces):
        fsend[n] = dot(pick[...], faces).astype(BF16).reshape(SLOTS, FACE_ROWS, LOADS)

    def send_faces(n):
        for w, move in enumerate(MOVES):
            span = pl.ds(w * CAP, CAP)
            remote(fsend.at[n, span], farr.at[n, span], fs.at[n], fr.at[n], around[-move])

    def arrived(n):
        return farr[n].reshape(SLOT_ROWS, LOADS)

    def remainder(value):
        return (value - value.astype(BF16).astype(F32)).astype(BF16)

    fetches[0].wait()
    vz[...] = out[...].astype(BF16)
    pack(LAM_HI, vz[0:FACE_TOTAL, :])
    low[...] = remainder(out[0:FACE_TOTAL, :])
    pl.semaphore_wait(barrier, len(MOVES) + NL - 1 + NXY - 1)
    send_faces(LAM_HI)

    own_slot = []
    own_off = [face_offset[f, s] for f in range(FACES)]
    for f in range(FACES):
        rank = jnp.int32(0)
        for g in range(f):
            rank = rank + jnp.where(own_off[g] == own_off[f], 1, 0)
        own_slot.append(own_off[f] * CAP + rank)
        sign = (2 * face_sign[f, s] - 1).astype(F32)
        place[f * FACE_ROWS : (f + 1) * FACE_ROWS, :] = jnp.where(wide == own_slot[f], sign, 0.0).astype(BF16)
    for q in range(SLOTS):
        face = jnp.int32(0)
        for f in range(FACES):
            face = face + jnp.where(own_slot[f] == q, f, 0)
        leave[q * FACE_ROWS : (q + 1) * FACE_ROWS, :] = ones_where(narrow == face)

    def cut_coarse():
        fetches[2].wait()
        cpad[...] = jnp.zeros(cpad.shape, F32)
        for b in range(NX):
            cpad[b * 8 : b * 8 + MODES, :] = cinv[b * MODES : (b + 1) * MODES, :]
        half = cinv.shape[1] // 2
        stack = jnp.concatenate(parts_of(cpad[...], 3), axis=0).astype(BF16)
        row = iota((half, LOADS), 0)
        col = iota((half, LOADS), 1)
        want = jnp.where((col & 7) < MODES, (col >> 3) * (NX * MODES) + (col & 7), -NX * MODES)
        for xd in range(NX):
            choose = ones_where(row == want + xd * MODES)
            for h in range(2):
                got = dot(stack[:, h * half : (h + 1) * half], choose)
                csend[xd * 2 + h] = got[0:32] + got[32:64] + got[64:96]
                yd = 2 * x + h
                mine = (yd == y) & (x == xd)

                @pl.when(mine)
                def _():
                    pltpu.make_async_copy(csend.at[xd * 2 + h], cmat.at[y], kr).start()

                @pl.when(jnp.logical_not(mine))
                def _():
                    remote(csend.at[xd * 2 + h], cmat.at[y], ks, kr, (yd * NL + l, xd))

    def residual(rows_from, rows_to):
        g_hi, g_lo = parts_of(grad[rows_from:rows_to, :], 2)
        m = modes_rows[:, rows_from:rows_to]
        a = dot(m, g_hi.astype(BF16))
        b = dot(m, g_lo.astype(BF16))
        return a[0:8] + a[8:16] + b[0:8]

    def row_of_ones(t):
        return ones_where(iota((LOADS, LOADS), 0) == t)

    def step(t):
        if t == 0:
            cut_coarse()
            fetches[1].wait()
            m_pad = jnp.concatenate([modes[...], jnp.zeros((2, ORDER), F32)], axis=0)
            m_hi, m_lo = parts_of(m_pad, 2)
            modes_rows[...] = jnp.concatenate([m_hi, m_lo], axis=0).astype(BF16)
            fetches[4].wait()
            wait_bytes(fr.at[LAM_HI], farr.at[LAM_HI])
            came = dot(place[...], arrived(LAM_HI))
        else:
            vz[...] = out[...].astype(BF16)
            came = dot(place[...], lam_far[...].astype(BF16))
        vz[0:FACE_TOTAL, :] = (vz[0:FACE_TOTAL, :].astype(F32) + came).astype(BF16)
        ybf[...] = dot(dual[0, 0:FACE_TOTAL, :], vz[...]).astype(BF16)
        bsend[t] = dot(leave[...], ybf[...]).astype(BF16).reshape(SLOTS, FACE_ROWS, LOADS)
        for w, move in enumerate(MOVES):
            span = pl.ds(w * CAP, CAP)
            remote(bsend.at[t, span], barr.at[t, span], bs.at[t], br.at[t], around[move])
        if t == 0:
            fetches[5].wait()
            for b in range(FACES):
                hit = (wide >= 0) & (block_of == b)
                spread[b * FACE_ROWS : (b + 1) * FACE_ROWS, :] = jnp.where(hit, sign_of, 0.0).astype(BF16)
        y_rest = dot(dual[0, FACE_TOTAL:, :], vz[...]).astype(BF16).astype(F32)
        grad[FACE_TOTAL:, :] = y_rest - loads[FACE_TOTAL:, :]
        e_rest = residual(FACE_TOTAL, ORDER)
        y_less = ybf[...].astype(F32) - loads[0:FACE_TOTAL, :]
        wait_bytes(br.at[t], barr.at[t])
        grad[0:FACE_TOTAL, :] = y_less + dot(spread[...], barr[t].reshape(SLOT_ROWS, LOADS))
        eline[t, l] = e_rest + residual(0, FACE_TOTAL)

        for device in line:
            remote(eline.at[t, l], eline.at[t, l], es.at[t], er.at[t], device)
        if t == 0:
            m_all = jnp.concatenate([m_hi, m_hi, m_lo, jnp.zeros((8, ORDER), F32)], axis=0).astype(BF16)
            modes_cols[...] = dot_t(m_all, ones_where(iota((32, 32), 0) == iota((32, 32), 1))).astype(BF16)
            fetches[3].wait()
            con = jnp.concatenate([contact[...].astype(F32), jnp.zeros((16 - STEPS, ORDER), F32)], axis=0).astype(BF16)
            columns[...] = dot_t(con, ones_where(iota((16, LOADS), 0) == iota((16, LOADS), 1))).astype(BF16)
            wait_bytes(kr, cmat)
        wait_bytes(er.at[t], eline.at[t, pl.ds(0, NL - 1)])
        product = jnp.dot(
            cmat[...].reshape(NXY * 8, LOADS), eline[t].reshape(NL * 8, LOADS),
            precision=lax.Precision.HIGHEST, preferred_element_type=F32,
        )
        part[t] = product.reshape(NXY, 8, LOADS)
        for q, device in plane:
            remote(part.at[t, q], cpl.at[t, me], cs.at[t], cr.at[t], device)
        cpl[t, me] = part[t, me]
        if t == 0:
            pack(LAM_LO, low[...])
            send_faces(LAM_LO)
            pack(CONTACT, columns[0:FACE_TOTAL, :])
            send_faces(CONTACT)
            for i in range(STEPS):
                floor[i] = jnp.where(dot(columns[...], row_of_ones(i)) > 0.5, 0.0, LOW)
        wait_bytes(cr.at[t], cpl.at[t, pl.ds(0, NXY - 1)])
        c_hi, c_lo = parts_of(jnp.sum(cpl[t], axis=0), 2)
        c_all = jnp.concatenate([c_hi, c_lo, c_hi, jnp.zeros((8, LOADS), F32)], axis=0).astype(BF16)

        def correct(rows_from, rows_to):
            value = grad[rows_from:rows_to, :] - dot(modes_cols[rows_from:rows_to, :], c_all)
            dirn[rows_from:rows_to, :] = value
            vz[rows_from:rows_to, :] = value.astype(BF16)

        correct(0, FACE_TOTAL)
        pack(DIR_HI + t, vz[0:FACE_TOTAL, :])
        send_faces(DIR_HI + t)
        correct(FACE_TOTAL, ORDER)
        slope = jnp.sum(grad[...] * dirn[...], axis=0, keepdims=True)
        image[...] = dot(dual[0, :, FACE_TOTAL:], vz[FACE_TOTAL:, :])

        wait_bytes(fr.at[DIR_HI + t], farr.at[DIR_HI + t])
        z = vz[0:FACE_TOTAL, :].astype(F32) + dot(place[...], arrived(DIR_HI + t))
        zf[...] = z
        whole = image[...] + dot(dual[0, :, 0:FACE_TOTAL], z.astype(BF16))
        curv = jnp.sum(zf[...] * whole[0:FACE_TOTAL], axis=0, keepdims=True)
        curv = curv + jnp.sum(dirn[FACE_TOTAL:, :] * whole[FACE_TOTAL:], axis=0, keepdims=True)
        arl[t, l] = jnp.concatenate([slope, curv], axis=0)
        for device in line:
            remote(arl.at[t, l], arl.at[t, l], als.at[t], alr.at[t], device)
        last = t == STEPS - 1
        if not last:
            pack(DIR_LO + t, remainder(dirn[0:FACE_TOTAL, :]))
            send_faces(DIR_LO + t)
        wait_bytes(alr.at[t], arl.at[t, pl.ds(0, NL - 1)])
        arp[t, me] = jnp.sum(arl[t], axis=0)
        for _, device in plane:
            remote(arp.at[t, me], arp.at[t, me], aps.at[t], apr.at[t], device)

        if t == 0:
            wait_bytes(fr.at[LAM_LO], farr.at[LAM_LO])
            wait_bytes(fr.at[CONTACT], farr.at[CONTACT])
            lam_far[...] = arrived(LAM_HI).astype(F32) + arrived(LAM_LO).astype(F32)
            for i in range(STEPS - 1):
                floor_far[i] = jnp.where(dot(arrived(CONTACT), row_of_ones(i)) > 0.5, 0.0, LOW)
        if not last:
            wait_bytes(fr.at[DIR_LO + t], farr.at[DIR_LO + t])
        wait_bytes(apr.at[t], arp.at[t, pl.ds(0, NXY - 1)])
        total = jnp.sum(arp[t], axis=0)
        alpha = total[0:1] / total[1:2]
        if not last:
            dirn_far = arrived(DIR_HI + t).astype(F32) + arrived(DIR_LO + t).astype(F32)
            lam_far[...] = jnp.maximum(lam_far[...] - alpha * dirn_far, floor_far[t])
        out[...] = jnp.maximum(out[...] - alpha * dirn[...], floor[t])

    for t in range(STEPS):
        step(t)

    for n in range(MESSAGES):
        wait_bytes(fs.at[n], fsend.at[n])
    for t in range(STEPS):
        wait_bytes(bs.at[t], bsend.at[t])
        wait_bytes(es.at[t], eline.at[t, pl.ds(0, NL - 1)])
        wait_bytes(cs.at[t], part.at[t, pl.ds(0, NXY - 1)])
        wait_bytes(als.at[t], arl.at[t, pl.ds(0, NL - 1)])
        wait_bytes(aps.at[t], arp.at[t, pl.ds(0, NXY - 1)])
    own_cut = x == y // 2

    @pl.when(own_cut)
    def _():
        wait_bytes(ks, csend.at[pl.ds(0, 7)])

    @pl.when(jnp.logical_not(own_cut))
    def _():
        wait_bytes(ks, csend)


def on_device(lam_start, loads, dual_ops, modes, coarse_inverse, face_offset, face_block, face_sign, contact):
    tables = [face[:, 0, :].T for face in (face_offset, face_block, face_sign)]
    whole = pl.BlockSpec(memory_space=pl.ANY)
    smem = pl.BlockSpec(memory_space=pltpu.SMEM)
    vmem, dma = pltpu.VMEM, pltpu.SemaphoreType.DMA
    return pl.pallas_call(
        kernel,
        name="dual_steps",
        out_shape=jax.ShapeDtypeStruct(lam_start.shape, F32),
        in_specs=[smem] * 3 + [whole] * 6,
        out_specs=pl.BlockSpec(memory_space=pltpu.VMEM),
        scratch_shapes=[
            vmem(loads.shape, F32),
            vmem(dual_ops.shape, BF16),
            vmem(modes.shape, F32),
            vmem(coarse_inverse.shape, F32),
            vmem(contact.shape, jnp.int32),
            vmem((FACE_TOTAL, SLOT_ROWS), BF16),
            vmem((SLOT_ROWS, FACE_TOTAL), BF16),
            vmem((SLOT_ROWS, FACE_TOTAL), BF16),
            vmem((FACE_TOTAL, SLOT_ROWS), BF16),
            vmem((ORDER, LOADS), BF16),
            vmem((FACE_TOTAL, LOADS), BF16),
            vmem((FACE_TOTAL, LOADS), BF16),
            vmem((FACE_TOTAL, LOADS), F32),
            vmem((ORDER, LOADS), F32),
            vmem((ORDER, LOADS), F32),
            vmem((ORDER, LOADS), F32),
            vmem((SLOT_ROWS, LOADS), F32),
            vmem((16, ORDER), BF16),
            vmem((ORDER, 32), BF16),
            vmem((ORDER, LOADS), BF16),
            vmem((STEPS, ORDER, LOADS), F32),
            vmem((STEPS - 1, SLOT_ROWS, LOADS), F32),
            vmem((MESSAGES, SLOTS, FACE_ROWS, LOADS), BF16),
            vmem((MESSAGES, SLOTS, FACE_ROWS, LOADS), BF16),
            vmem((STEPS, SLOTS, FACE_ROWS, LOADS), BF16),
            vmem((STEPS, SLOTS, FACE_ROWS, LOADS), BF16),
            vmem((STEPS, NL, 8, LOADS), F32),
            vmem((STEPS, NXY, 8, LOADS), F32),
            vmem((STEPS, NXY, 8, LOADS), F32),
            vmem((STEPS, NL, 2, LOADS), F32),
            vmem((STEPS, NXY, 2, LOADS), F32),
            vmem((8, 32, LOADS), F32),
            vmem((8, 32, LOADS), F32),
            vmem((32, coarse_inverse.shape[1]), F32),
            dma((6,)),
            dma((MESSAGES,)),
            dma((MESSAGES,)),
        ]
        + [dma((STEPS,))] * 10
        + [dma, dma],
        compiler_params=pltpu.CompilerParams(collective_id=1, has_side_effects=True),
    )(*tables, lam_start, loads, dual_ops, modes, coarse_inverse, contact)


def solution(mesh):
    both = ("sub", "grp")
    placed = (
        P(both, None),
        P(both, None),
        P(both, None, None),
        P(None, both),
        P("sub", "grp"),
        P(None, "grp", None),
        P(None, "grp", None),
        P(None, "grp", None),
        P(None, both),
    )
    return jax.shard_map(on_device, mesh=mesh, in_specs=placed, out_specs=P(both, None), check_vma=False)
```

time: 143 us -> 126 us (0.88)
  Pallas kernels: 141 us -> 124 us
    pallas_call x1, Pallas kernels: 141 us -> 124 us  [on_device(): pl.pallas_call(kernel, name='dual_steps', out_shape=jax.ShapeDtypeStruct(...]
where the time goes in v2:
time: 126 us
  Pallas kernels  124 us (98%)
  local copies, waits for them, and re-layouts  1.87 us (1%)
    pallas_call x1, Pallas kernels, on_device(): pl.pallas_call(kernel, name='dual_steps', out_shape=jax.ShapeDtypeStruct(...  124 us

profile of v2, /device:TPU:1, one launch (start us, length us, event | category | flops | bytes accessed | tf_op | source)
XLA Modules:
  0.0 125.6 jit_solution(4177678479867868102)
XLA Ops:
  0.0 123.8 %dual_steps.1 = f32[1024,128]{1,0:T(8,128)} custom-call(s32[8,128]{1,0:T(8,128)} %bitcast.9, s32[8,128]{1,0:T(8,128)} %bitcast.10, s32[8,128]{1,0:T(8,128)} %bitcast.11, f32[1024,128]{1,0:T(8,128)} %lam_hbm.1, f32[1024,128]{1,0:T(8,128)} %loads_hbm.1, bf16[1,1024,1024]{2,1,0:T(8,128)(2,1)} %dual_hbm.1, f32[6,1024]{1,0:T(8,128)} %modes_hbm.1, ...), custom_call_target="tpu_custom_call" | custom-call | tf_op jit(solution)/shard_map/dual_steps/pallas_call | solution.py:335
  123.8 1.9 %copy.11 = f32[1024,128]{1,0:T(8,128)} copy(f32[1024,128]{1,0:T(8,128)} %dual_steps.1) | data formatting | bytes 1048576
